TPU v7x, 128 devices: a whole 4x4x4 slice. The times are simulated.
128 devices in a mesh: wide: 16 (over x_lo, y, core), narrow: 8 (over z, x_hi).
Axes of the slice: x: 4 (x_hi: 2, x_lo: 2; x = x_hi * 2 + x_lo), y: 4, z: 4, core: 2. Of those that a mesh axis runs over, the one named last changes fastest.
Arguments:
- clip_tokens: bfloat16 [256, 256, 1152], P(('wide', 'narrow')), may hold values from -6 to 6
- cotangent: bfloat16 [256, 256, 1152], P(None, ('wide', 'narrow')), may hold values from -24 to 24
- qkv_spatial: bfloat16 [1152, 1728], replicated, may hold values from -0.1875 to 0.1875
- proj_spatial: bfloat16 [1152, 576], replicated, may hold values from -0.25 to 0.25
- adaln_spatial: float32 [3, 1152], replicated, may hold values from -4 to 4
- qknorm_spatial: float32 [2, 72], replicated, may hold values from 0.5 to 2.5
- qkv_temporal: bfloat16 [1152, 1728], replicated, may hold values from -0.1875 to 0.1875
- proj_temporal: bfloat16 [1152, 576], replicated, may hold values from -0.25 to 0.25
- adaln_temporal: float32 [3, 1152], replicated, may hold values from -4 to 4
- qknorm_temporal: float32 [2, 72], replicated, may hold values from 0.5 to 2.5
Outputs:
- result: bfloat16 [256, 256, 1152], P(None, ('wide', 'narrow'))
- grad_clip: bfloat16 [256, 256, 1152], P(('wide', 'narrow'))
- grad_qkv_spatial: float32 [1152, 1728], P(('wide', 'narrow'))
- grad_proj_spatial: float32 [1152, 576], P(('wide', 'narrow'))
- grad_qkv_temporal: float32 [1152, 1728], P(('wide', 'narrow'))
- grad_proj_temporal: float32 [1152, 576], P(('wide', 'narrow'))
All inputs are finite; a program needn't handle non-finite values.
Results may differ from a plain program's by a relative error of at most 0.015.
The roundings to bfloat16 on the way count: a program that leaves them out, or rounds other values in their place, can miss the bound.
Values may be sent and summed in bfloat16 or wider, within the bound.
A program may use at most 192 MiB of HBM per device.

v0:
```python
import functools
import math

import jax
import jax.numpy as jnp
from jax import lax
from jax.experimental import pallas as pl
from jax.experimental.pallas import tpu as pltpu
from jax.sharding import PartitionSpec as P

HDIM = 72
HEADS = 8
HD = HDIM * HEADS
MODEL = 1152
LANE_TILES = MODEL // 128
TOKENS = 512
SEQ = 256
EPSILON = 1e-06
QKV_TILES, PROJ_TILES = 14, 5
SHARDS = 128
MESSAGE = 40
NT = (((1,), (1,)), ((), ()))
TN = (((0,), (0,)), ((), ()))
F32, BF16 = jnp.float32, jnp.bfloat16
MESH = pl.DeviceIdType.MESH
PARTS = ((0, 7, 64, ("y", "z", "x")), (7, 7, 64, ("z", "x", "y")), (14, 5, 48, ("x", "y", "z")))
COUNT = len(PARTS)


def place():
    wide = lax.axis_index("wide")
    narrow = lax.axis_index("narrow")
    x_lo, y, core = wide // 8, (wide // 2) % 4, wide % 2
    z, x_hi = narrow // 2, narrow % 2
    return {"x": x_hi * 2 + x_lo, "y": y, "z": z, "core": core}


def device_of(at):
    wide = (at["x"] % 2) * 8 + at["y"] * 2 + at["core"]
    narrow = at["z"] * 2 + at["x"] // 2
    return (wide, narrow)


def moved(at, axis, step):
    size = 2 if axis == "core" else 4
    return {**at, axis: (at[axis] + step) % size}


def row_loop(total, step, body, unroll=1):
    lax.fori_loop(0, total // step, lambda i, c: (body(pl.ds(pl.multiple_of(i * step, step), step)), c)[1], 0,
                  unroll=unroll)


def flat_rows(ref):
    return lambda rows: ref[rows, :].astype(F32)


def tile_rows(ref):
    return lambda rows: jnp.concatenate(
        [ref[pl.ds(pl.multiple_of(t * TOKENS + rows.start, 8), rows.size), :] for t in range(LANE_TILES)], axis=1)


def put_tiles(ref, rows, value):
    for t in range(LANE_TILES):
        ref[pl.ds(pl.multiple_of(t * TOKENS + rows.start, 8), rows.size), :] = value[:, t * 128:t * 128 + 128]


def centred(x):
    centre = x - jnp.mean(x, axis=-1, keepdims=True)
    spread = jnp.mean(centre * centre, axis=-1, keepdims=True)
    scale = lax.rsqrt(spread + EPSILON)
    return centre * scale, scale


def norm_tokens(x, adaln, normed):
    def body(rows):
        hat, _ = centred(x(rows))
        normed[rows, :] = (hat * (1.0 + adaln[1:2, :]) + adaln[0:1, :]).astype(BF16)

    row_loop(TOKENS, 16, body, 4)


def project_qkv(weight_t, normed, qkv_t):
    def body(i, carry):
        rows = pl.ds(pl.multiple_of(i * 576, 64), 576)
        qkv_t[rows, :] = lax.dot_general(weight_t[rows, :], normed[...], NT, preferred_element_type=F32)
        return carry

    lax.fori_loop(0, 3, body, 0)


def gate_cotangent(cot, adaln, branch):
    def body(rows):
        branch[rows, :] = (adaln[2:3, :] * cot(rows)).astype(BF16)

    row_loop(TOKENS, 64, body)


def pull_mixed(proj_t, branch, dmixed_t):
    dmixed_t[...] = lax.dot_general(proj_t[...], branch[...], NT, preferred_element_type=F32)


def column(row):
    grid = (HDIM, HDIM)
    same = lax.broadcasted_iota(jnp.int32, grid, 0) == lax.broadcasted_iota(jnp.int32, grid, 1)
    return jnp.sum(jnp.where(same, jnp.broadcast_to(row, grid), 0.0), axis=1, keepdims=True)


def split3(value):
    high = value.astype(BF16).astype(F32)
    return high, value - high


def heads_loop(qkv_t, gains, mixed_t, dmixed_t):
    root = 1.0 / math.sqrt(HDIM)
    q_gain, k_gain = column(gains[0:1, :]), column(gains[1:2, :])

    def body(index, carry):
        head, seq = index // 2, index % 2
        lanes = pl.ds(pl.multiple_of(seq * SEQ, SEQ), SEQ)
        at = [pl.ds(pl.multiple_of(part * HD + head * HDIM, 8), HDIM) for part in range(3)]
        q, k, v = (qkv_t[rows, lanes] for rows in at)
        q_scale = lax.rsqrt(jnp.mean(q * q, axis=0, keepdims=True) + EPSILON)
        k_scale = lax.rsqrt(jnp.mean(k * k, axis=0, keepdims=True) + EPSILON)
        q_hat, k_hat = q * q_scale, k * k_scale
        qs, kn = q_hat * (q_gain * root), k_hat * k_gain
        q_high, q_low = split3(qs)
        k_high, k_low = split3(kn)
        q3 = jnp.concatenate([q_high, q_low, q_high], axis=0).astype(BF16)
        k3 = jnp.concatenate([k_high, k_high, k_low], axis=0).astype(BF16)
        raised = jnp.exp(lax.dot_general(k3, q3, TN, preferred_element_type=F32))
        inverse = 1.0 / jnp.sum(raised, axis=0, keepdims=True)
        v_low = v.astype(BF16)
        if mixed_t is not None:
            out = jnp.dot(v_low, raised.astype(BF16), preferred_element_type=F32) * inverse
            mixed_t[at[0], lanes] = out
        if dmixed_t is not None:
            weights = raised * inverse
            d_out = dmixed_t[at[0], lanes].astype(BF16)
            d_weights = lax.dot_general(v_low, d_out, TN, preferred_element_type=F32)
            shift = jnp.sum(weights * d_weights, axis=0, keepdims=True)
            d_scores = (weights * (d_weights - shift)).astype(BF16)
            dv = lax.dot_general(d_out, weights.astype(BF16), NT, preferred_element_type=F32)
            dq = jnp.dot(k_high.astype(BF16), d_scores, preferred_element_type=F32)
            dk = lax.dot_general(q_high.astype(BF16), d_scores, NT, preferred_element_type=F32)
            dq = dq * (q_gain * root)
            dk = dk * k_gain
            qkv_t[at[0], lanes] = q_scale * (dq - q_hat * jnp.mean(q_hat * dq, axis=0, keepdims=True))
            qkv_t[at[1], lanes] = k_scale * (dk - k_hat * jnp.mean(k_hat * dk, axis=0, keepdims=True))
            qkv_t[at[2], lanes] = dv
        return carry

    lax.fori_loop(0, 2 * HEADS, body, 0, unroll=2)


def wide_rows(source, used, ref):
    ref[:, :used] = source[...].T.astype(BF16)
    ref[:, used:] = jnp.zeros((TOKENS, ref.shape[1] - used), BF16)


def add_projection(x, mixed, proj_t, adaln, put):
    def body(rows):
        projected = jnp.dot(mixed[rows, :HD], proj_t[...], preferred_element_type=F32)
        put(rows, x(rows) + adaln[2:3, :] * projected)

    row_loop(TOKENS, 256, body)


def pull_norm(x, cot, dqkv, weight_t, adaln, work, put):
    third = MODEL // 3
    for i in range(3):
        work[i * TOKENS:(i + 1) * TOKENS, :third] = jnp.dot(
            dqkv[:, :3 * HD], weight_t[:, i * third:(i + 1) * third], preferred_element_type=F32)

    def body(rows):
        d_normed = jnp.concatenate(
            [work[pl.ds(pl.multiple_of(i * TOKENS + rows.start, 8), rows.size), :third] for i in range(3)], axis=1)
        hat, scale = centred(x(rows))
        u = d_normed * (1.0 + adaln[1:2, :])
        d_x = scale * (u - jnp.mean(u, axis=-1, keepdims=True) - hat * jnp.mean(u * hat, axis=-1, keepdims=True))
        put(rows, cot(rows) + d_x)

    row_loop(TOKENS, 16, body, 4)


def gradient_part(left, right, first_tile, tiles, slab, work):
    done = 0
    while done < tiles:
        size = min(2, tiles - done)
        lane = pl.multiple_of((first_tile + done) * 128, 128)
        out = jnp.dot(left[...], right[:, pl.ds(lane, size * 128)], preferred_element_type=F32)
        for t in range(size):
            work[(done + t) * MODEL:(done + t + 1) * MODEL, :] = out[:, t * 128:(t + 1) * 128]
        done += size
    skip = max(0, 8 - tiles)

    def gather(s, carry):
        rows = [work[pl.ds(t * MODEL + 9 * s, 8), :] for t in range(tiles)]
        rows.append(work[pl.ds(9 * s + 8, 8, stride=MODEL), :])
        slab[s // 64, (s // 16) % 4, (s // 8) % 2, (s // 2) % 4, s % 2] = jnp.concatenate(rows, axis=0).astype(BF16)
        return carry

    lax.fori_loop(0, SHARDS, gather, 0, unroll=2)


def pack_messages(source, send):
    top = lax.broadcasted_iota(jnp.int32, (8, 128), 0) < 2

    def body(s, carry):
        rows = [source[pl.ds(a * SEQ + 2 * s + b, 8, stride=TOKENS), :] for a in range(2) for b in range(2)]
        last = 8 * TOKENS + 2 * s
        rows.append(jnp.where(top, source[pl.ds(last, 8), :], source[pl.ds(last + SEQ - 2, 8), :]))
        send[s] = jnp.concatenate(rows, axis=0).astype(BF16)
        return carry

    lax.fori_loop(0, SHARDS, body, 0, unroll=4)


def unpack_messages(recv, target):
    def body(s, carry):
        rows = recv[s].astype(F32)
        for a in range(2):
            for b in range(2):
                at = (a * 2 + b) * 8
                target[pl.ds(b * SEQ + 2 * s + a, 8, stride=TOKENS), :] = rows[at:at + 8]
            target[pl.ds(8 * TOKENS + 2 * s + a, 2, stride=SEQ), :] = rows[32 + 2 * a:34 + 2 * a]
        return carry

    lax.fori_loop(0, SHARDS, body, 0, unroll=4)


def start_exchange(me, send, recv, send_sem, recv_sem, own_sem):
    def body(step, carry):
        other = (me + step) % SHARDS
        pltpu.make_async_remote_copy(
            src_ref=send.at[other], dst_ref=recv.at[me], send_sem=send_sem, recv_sem=recv_sem,
            device_id=(other // 8, other % 8), device_id_type=MESH).start()
        return carry

    lax.fori_loop(1, SHARDS, body, 0)
    own = pltpu.make_async_copy(send.at[me], recv.at[me], own_sem)
    own.start()
    every = pltpu.make_async_remote_copy(
        src_ref=send.at[pl.ds(0, SHARDS - 1)], dst_ref=recv.at[pl.ds(0, SHARDS - 1)],
        send_sem=send_sem, recv_sem=recv_sem, device_id=((me + 1) % SHARDS // 8, (me + 1) % SHARDS % 8),
        device_id_type=MESH)
    return own, every


def add_rows(count, target, sources):
    def step(index, carry):
        total = sources[0](index).astype(F32)
        for source in sources[1:]:
            total = total + source(index).astype(F32)
        target(index, total.astype(BF16))
        return carry

    lax.fori_loop(0, count, step, 0)


class Scatter:
    def __init__(self, at, slabs, buffers, sems, base, sums, which, scale):
        self.at, self.slabs, self.sums, self.which, self.scale = at, slabs, sums, which, scale
        self.from_core, self.first, self.second, self.third, *recvs = [
            buffers[i * COUNT:(i + 1) * COUNT] for i in range(7)]
        self.bufs, self.recvs = (self.first, self.second, self.third), recvs
        self.send_sem, self.recv_sem = sems
        self.base = base
        self.core, self.flying = {}, {}

    def copy(self, key, slot, src, dst, axis, step):
        slot = self.base + slot
        made = pltpu.make_async_remote_copy(
            src_ref=src, dst_ref=dst, send_sem=self.send_sem.at[slot], recv_sem=self.recv_sem.at[slot],
            device_id=device_of(moved(self.at, axis, step)), device_id_type=MESH)
        made.start()
        self.flying[key] = made

    def begin(self, part):
        self.copy((part, "core"), COUNT * 18 + part, self.slabs[part].at[:, :, 1 - self.at["core"]],
                  self.from_core[part], "core", 1)

    def join_cores(self, part):
        self.flying[(part, "core")].wait_recv()
        order, first = PARTS[part][3], self.first[part]
        mine, theirs, core = self.slabs[part], self.from_core[part], self.at["core"]

        def target(i, value):
            digit = {"x": (i % 2) * 2 + i // 32, "y": (i // 8) % 4, "z": (i // 2) % 4}
            first[digit[order[0]], digit[order[1]], digit[order[2]]] = value

        add_rows(64, target, [lambda i: mine[i // 32, (i // 8) % 4, core, (i // 2) % 4, i % 2],
                              lambda i: theirs[i // 32, (i // 8) % 4, (i // 2) % 4, i % 2]])
        self.start(part, 0)

    @staticmethod
    def halves(level, block):
        cut = 2 if level < 2 else 32
        return block.at[0:cut], block.at[cut:block.shape[0]]

    def start(self, part, level):
        axis = PARTS[part][3][level]
        here, source, recv = self.at[axis], self.bufs[level][part], self.recvs[level][part]
        for direction in (0, 1):
            step = 3 if direction else 1
            relay, plain = direction, 1 - direction
            far, near = source.at[(here + 2) % 4], source.at[(here + step) % 4]
            slot = ((part * 3 + level) * 2 + direction) * 3
            self.copy((part, level, direction, 0), slot, self.halves(level, far)[relay],
                      self.halves(level, recv.at[direction, 0])[relay], axis, step)
            self.copy((part, level, direction, 1), slot + 1, self.halves(level, near)[plain],
                      self.halves(level, recv.at[direction, 1])[plain], axis, step)

    def relay(self, part, level):
        axis = PARTS[part][3][level]
        here, source, recv = self.at[axis], self.bufs[level][part], self.recvs[level][part]
        for direction in (0, 1):
            step = 3 if direction else 1
            self.flying[(part, level, direction, 0)].wait_recv()
            near = self.halves(level, source.at[(here + step) % 4])[direction]
            came = self.halves(level, recv.at[direction, 0])[direction]
            if level == 0:
                def target(i, v):
                    came[i // 4, i % 4] = v
                add_rows(8, target, [lambda i: came[i // 4, i % 4], lambda i: near[i // 4, i % 4]])
            elif level == 1:
                def target(i, v):
                    came[i] = v
                add_rows(2, target, [lambda i: came[i], lambda i: near[i]])
            else:
                came[...] = (came[...].astype(F32) + near[...].astype(F32)).astype(BF16)
            slot = ((part * 3 + level) * 2 + direction) * 3 + 2
            self.copy((part, level, direction, 2), slot, came, self.halves(level, recv.at[direction, 1])[direction],
                      axis, step)

    def finish(self, part, level):
        axis = PARTS[part][3][level]
        source, recv = self.bufs[level][part].at[self.at[axis]], self.recvs[level][part]
        for direction in (0, 1):
            self.flying[(part, level, direction, 1)].wait_recv()
            self.flying[(part, level, direction, 2)].wait_recv()
        plus, minus = recv.at[0, 1], recv.at[1, 1]
        if level == 0:
            goal = self.second[part]

            def target(i, v):
                goal[i // 4, i % 4] = v
            add_rows(16, target, [lambda i: source[i // 4, i % 4], lambda i: plus[i // 4, i % 4],
                                  lambda i: minus[i // 4, i % 4]])
        elif level == 1:
            goal = self.third[part]

            def target(i, v):
                goal[i] = v
            add_rows(4, target, [lambda i: source[i], lambda i: plus[i], lambda i: minus[i]])
        else:
            start = sum(p[2] for p in PARTS[:part])
            self.sums[self.which, start:start + PARTS[part][2], :] = (
                source[...].astype(F32) + plus[...].astype(F32) + minus[...].astype(F32)) * self.scale
        if level < 2:
            self.start(part, level + 1)

    def drain(self):
        for made in self.flying.values():
            made.wait_send()


def parts_step(step, *level):
    for part in range(COUNT):
        step(part, *level)


def both_blocks(scale, clip_hbm, cot_hbm, wt_s_hbm, pt_s_hbm, adaln_s, gains_s, wt_t_hbm, pt_t_hbm, adaln_t, gains_t,
                result, grad_clip, sums,
                clip, cot, wt_s, pt_s, wt_t, pt_t, normed_s, normed_t, branch, qkv_s, qkv_t, mixed_f, dmixed_f,
                mixed_s, mixed_t, dqkv, left, work, tokens_a, tokens_b, send, recv_a, recv_b, slab0, slab1, slab2,
                *rest):
    buffers = rest[:7 * COUNT]
    load_sem, own_sem, send_a, send_b, got_a, got_b, sum_send, sum_recv, free_sem = rest[7 * COUNT:]
    at = place()
    me = lax.axis_index("wide") * 8 + lax.axis_index("narrow")
    loads = []
    for i, (hbm, vmem) in enumerate(((clip_hbm, clip), (wt_s_hbm, wt_s), (pt_s_hbm, pt_s), (cot_hbm, cot),
                                     (pt_t_hbm, pt_t), (wt_t_hbm, wt_t))):
        load = pltpu.make_async_copy(hbm, vmem, load_sem.at[i])
        load.start()
        loads.append(load)
    barrier = pltpu.get_barrier_semaphore()

    def greet(step, carry):
        other = (me + step) % SHARDS
        pl.semaphore_signal(barrier, inc=1, device_id=(other // 8, other % 8), device_id_type=MESH)
        return carry

    lax.fori_loop(1, SHARDS, greet, 0)

    loads[0].wait()
    norm_tokens(flat_rows(clip), adaln_s, normed_s)
    loads[1].wait()
    project_qkv(wt_s, normed_s, qkv_s)
    heads_loop(qkv_s, gains_s, mixed_f, None)
    wide_rows(mixed_f, HD, mixed_s)
    loads[2].wait()
    add_projection(flat_rows(clip), mixed_s, pt_s, adaln_s, functools.partial(put_tiles, tokens_a))
    pack_messages(tokens_a, send)
    pl.semaphore_wait(barrier, SHARDS - 1)
    own, every = start_exchange(me, send, recv_a, send_a, got_a, own_sem.at[0])

    loads[3].wait()
    gate_cotangent(flat_rows(cot), adaln_t, branch)
    loads[4].wait()
    pull_mixed(pt_t, branch, dmixed_f)
    loads[5].wait()
    own.wait()
    every.wait_recv()
    unpack_messages(recv_a, tokens_b)
    middle = tile_rows(tokens_b)
    norm_tokens(middle, adaln_t, normed_t)
    project_qkv(wt_t, normed_t, qkv_t)
    heads_loop(qkv_t, gains_t, mixed_f, dmixed_f)
    wide_rows(qkv_t, 3 * HD, dqkv)
    pull_norm(middle, flat_rows(cot), dqkv, wt_t, adaln_t, qkv_t, functools.partial(put_tiles, tokens_a))
    every.wait_send()
    pack_messages(tokens_a, send)
    own, every = start_exchange(me, send, recv_b, send_b, got_b, own_sem.at[1])
    wide_rows(mixed_f, HD, mixed_t)

    def put_result(rows, value):
        result[rows, :] = value.astype(BF16)

    slabs = (slab0, slab1, slab2)
    sems = (sum_send, sum_recv)
    sum_t = Scatter(at, slabs, buffers, sems, 0, sums, 1, scale)
    left[...] = normed_t[...].T
    for part in (0, 1):
        gradient_part(left, dqkv, PARTS[part][0], PARTS[part][1], slabs[part], work)
        sum_t.begin(part)
    left[...] = branch[...].T
    gradient_part(left, mixed_t, 0, PROJ_TILES, slabs[2], work)
    sum_t.begin(2)
    add_projection(middle, mixed_t, pt_t, adaln_t, put_result)

    own.wait()
    every.wait_recv()
    unpack_messages(recv_b, tokens_b)
    d_middle = tile_rows(tokens_b)
    gate_cotangent(d_middle, adaln_s, branch)
    pull_mixed(pt_s, branch, dmixed_f)
    parts_step(sum_t.join_cores)
    heads_loop(qkv_s, gains_s, None, dmixed_f)
    parts_step(sum_t.relay, 0)
    wide_rows(qkv_s, 3 * HD, dqkv)
    parts_step(sum_t.finish, 0)

    def put_grad(rows, value):
        grad_clip[rows, :] = value.astype(BF16)

    left[...] = normed_s[...].T
    parts_step(sum_t.relay, 1)
    pull_norm(flat_rows(clip), d_middle, dqkv, wt_s, adaln_s, qkv_s, put_grad)
    parts_step(sum_t.finish, 1)
    parts_step(sum_t.relay, 2)
    parts_step(sum_t.finish, 2)
    sum_t.drain()
    peers = [device_of(moved(at, "core", 1))] + [device_of(moved(at, a, d)) for a in ("x", "y", "z") for d in (1, 3)]
    for peer in peers:
        pl.semaphore_signal(free_sem, inc=1, device_id=peer, device_id_type=MESH)
    sum_s = Scatter(at, slabs, buffers, sems, COUNT * 19, sums, 0, scale)
    gradient_part(left, dqkv, PARTS[0][0], PARTS[0][1], slabs[0], work)
    pl.semaphore_wait(free_sem, len(peers))
    sum_s.begin(0)
    gradient_part(left, dqkv, PARTS[1][0], PARTS[1][1], slabs[1], work)
    sum_s.begin(1)
    sum_s.join_cores(0)
    left[...] = branch[...].T
    gradient_part(left, mixed_s, 0, PROJ_TILES, slabs[2], work)
    sum_s.begin(2)
    sum_s.join_cores(1)
    sum_s.join_cores(2)
    for level in range(3):
        parts_step(sum_s.relay, level)
        parts_step(sum_s.finish, level)
    sum_s.drain()
    every.wait_send()


def split_sums(sums, qkv_s, proj_s, qkv_t, proj_t):
    for which, outs in enumerate(((qkv_s, proj_s), (qkv_t, proj_t))):
        start = 0
        for first, tiles, rows, _ in PARTS:
            out, base = (outs[0], 0) if first < QKV_TILES else (outs[1], QKV_TILES)
            for t in range(tiles):
                lane = (first + t - base) * 128
                width = min(128, out.shape[1] - lane)
                out[0:8, lane:lane + width] = sums[which, start + 8 * t:start + 8 * t + 8, :width]
                ninth = start + 8 * tiles + t
                out[8:9, lane:lane + width] = sums[which, ninth:ninth + 1, :width]
            start += rows


def run_blocks(scale, clip, cot, wt_s, pt_s, adaln_s, gains_s, wt_t, pt_t, adaln_t, gains_t):
    token, qkv_f, heads_f = ((TOKENS, MODEL), BF16), ((3 * HD, TOKENS), F32), ((HD, TOKENS), F32)
    tiles = ((LANE_TILES * TOKENS, 128), F32)
    mixed, message = ((TOKENS, PROJ_TILES * 128), BF16), ((SHARDS, MESSAGE, 128), BF16)
    shapes = [token, token, ((3 * HD, MODEL), BF16), ((HD, MODEL), BF16), ((3 * HD, MODEL), BF16), ((HD, MODEL), BF16),
              token, token, token, qkv_f, qkv_f, heads_f, heads_f, mixed, mixed, ((TOKENS, QKV_TILES * 128), BF16),
              ((MODEL, TOKENS), BF16), ((8 * MODEL, 128), F32), ((LANE_TILES * TOKENS + 8, 128), F32), tiles, message, message, message]
    shapes += [((2, 4, 2, 4, 2, rows, 128), BF16) for _, _, rows, _ in PARTS]
    for lead in ((2, 4, 4, 2), (4, 4, 4), (4, 4), (4,), (2, 2, 4, 4), (2, 2, 4), (2, 2)):
        shapes += [(lead + (rows, 128), BF16) for _, _, rows, _ in PARTS]
    vmem, hbm = pl.BlockSpec(memory_space=pltpu.VMEM), pl.BlockSpec(memory_space=pl.ANY)
    return pl.pallas_call(
        functools.partial(both_blocks, scale),
        out_shape=[jax.ShapeDtypeStruct(*token), jax.ShapeDtypeStruct(*token), jax.ShapeDtypeStruct((2, 176, 128), F32)],
        in_specs=[hbm, hbm, hbm, hbm, vmem, vmem, hbm, hbm, vmem, vmem],
        out_specs=[vmem] * 3,
        scratch_shapes=[pltpu.VMEM(*s) for s in shapes] + [
            pltpu.SemaphoreType.DMA((6,)), pltpu.SemaphoreType.DMA((2,)),
            pltpu.SemaphoreType.DMA, pltpu.SemaphoreType.DMA, pltpu.SemaphoreType.DMA, pltpu.SemaphoreType.DMA,
            pltpu.SemaphoreType.DMA((2 * COUNT * 19,)), pltpu.SemaphoreType.DMA((2 * COUNT * 19,)),
            pltpu.SemaphoreType.REGULAR],
        compiler_params=pltpu.CompilerParams(collective_id=0, has_side_effects=True, vmem_limit_bytes=67043328),
        name="both_blocks",
    )(clip, cot, wt_s, pt_s, adaln_s, gains_s, wt_t, pt_t, adaln_t, gains_t)


def body(clip_tokens, cotangent, qkv_spatial, proj_spatial, adaln_spatial, qknorm_spatial,
         qkv_temporal, proj_temporal, adaln_temporal, qknorm_temporal):
    clip = clip_tokens.reshape(TOKENS, MODEL)
    cot = jnp.transpose(cotangent, (1, 0, 2)).reshape(TOKENS, MODEL)
    result, grad_clip, sums = run_blocks(
        1.0 / math.sqrt(SEQ * SEQ), clip, cot, qkv_spatial.T, proj_spatial.T, adaln_spatial, qknorm_spatial,
        qkv_temporal.T, proj_temporal.T, adaln_temporal, qknorm_temporal)
    grads = pl.pallas_call(
        split_sums,
        out_shape=[jax.ShapeDtypeStruct((9, 3 * HD), F32), jax.ShapeDtypeStruct((9, HD), F32)] * 2,
        in_specs=[pl.BlockSpec(memory_space=pltpu.VMEM)],
        out_specs=[pl.BlockSpec(memory_space=pltpu.VMEM)] * 4,
        name="split_sums",
    )(sums)
    result = jnp.transpose(result.reshape(2, SEQ, MODEL), (1, 0, 2))
    return (result, grad_clip.reshape(2, SEQ, MODEL), *grads)


def solution(mesh):
    in_specs = (
        P(("wide", "narrow"), None, None),
        P(None, ("wide", "narrow"), None),
        P(),
        P(),
        P(),
        P(),
        P(),
        P(),
        P(),
        P(),
    )
    out_specs = (
        P(None, ("wide", "narrow"), None),
        P(("wide", "narrow"), None, None),
        P(("wide", "narrow"), None),
        P(("wide", "narrow"), None),
        P(("wide", "narrow"), None),
        P(("wide", "narrow"), None),
    )
    return jax.shard_map(body, mesh=mesh, in_specs=in_specs, out_specs=out_specs, check_vma=False)
```

profile of v0, /device:TPU:0, one launch (start us, length us, event | category | flops | bytes accessed | tf_op | source)
XLA Modules:
  0.0 183.3 jit_solution(8322987152873574381)
XLA Ops:
  0.6 2.4 %copy.16 = bf16[2,256,1152]{2,1,0:T(8,128)(2,1)} copy(bf16[2,256,1152]{2,0,1:T(2,128)(2,1)} %bitcast.18) | data formatting | bytes 2359296 | tf_op jit(solution)/shard_map/transpose | solution.py:530
  3.0 174.0 %both_blocks.1 = (bf16[512,1152]{1,0:T(8,128)(2,1)}, bf16[512,1152]{1,0:T(8,128)(2,1)}, f32[2,176,128]{2,1,0:T(8,128)}) custom-call(bf16[512,1152]{1,0:T(8,128)(2,1)} %bitcast.17, bf16[512,1152]{1,0:T(8,128)(2,1)} %bitcast.12, bf16[1728,1152]{1,0:T(8,128)(2,1)} %bitcast.13, bf16[576,1152]{1,0:T(8,128)(2,1)} %bitcast.15, f32[3,1152]{1,0:T(4,128)} %adaln_s.1, ...), custom_call_target="tpu_custom_call" | custom-call | tf_op jit(solution)/shard_map/both_blocks/pallas_call | solution.py:512
  177.1 0.0 copy-start
  177.1 3.6 %copy.19 = bf16[2,256,1152]{2,0,1:T(2,128)(2,1)} copy(bf16[2,256,1152]{2,1,0:T(8,128)(2,1)} %bitcast.21) | data formatting | bytes 2359296 | tf_op jit(solution)/shard_map/reshape | solution.py:541
  180.7 1.6 split_sums.1
  182.3 0.0 copy-done
  182.3 1.0 copy.21
Async XLA Ops:
  177.1 5.2 %copy-start = (bf16[512,1152]{1,0:T(8,128)(2,1)S(1)}, bf16[512,1152]{1,0:T(8,128)(2,1)}, u32[]{:S(2)}) copy-start(bf16[512,1152]{1,0:T(8,128)(2,1)} %get-tuple-element.14) | copy-start | bytes 3538948
where the time goes:
time: 184 us; the launch traced here: 183 us
  Pallas kernels  176 us (96%)
  local copies, waits for them, and re-layouts  7.02 us (4%)
    pallas_call x1, Pallas kernels, run_blocks(): pl.pallas_call(functools.partial(both_blocks, scale), out_shape=[jax.Shap...  174 us

commit v1 on v0

--- a/solution.py
+++ b/solution.py
@@ -111,15 +111,20 @@
     return high, value - high
 
 
-def heads_loop(qkv_t, gains, mixed_t, dmixed_t):
+def heads_loop(qkv_t, gains, mixed_t, dmixed_t, first=0, last=2, unroll=1):
     root = 1.0 / math.sqrt(HDIM)
     q_gain, k_gain = column(gains[0:1, :]), column(gains[1:2, :])
 
-    def body(index, carry):
-        head, seq = index // 2, index % 2
+    def one(head, seq):
         lanes = pl.ds(pl.multiple_of(seq * SEQ, SEQ), SEQ)
         at = [pl.ds(pl.multiple_of(part * HD + head * HDIM, 8), HDIM) for part in range(3)]
-        q, k, v = (qkv_t[rows, lanes] for rows in at)
+        loaded = [qkv_t[rows, lanes] for rows in at]
+        loaded.append(None if dmixed_t is None else dmixed_t[at[0], lanes])
+        return at, lanes, loaded
+
+    def compute(at, lanes, loaded):
+        q, k, v, d_mixed = loaded
+        stores = []
         q_scale = lax.rsqrt(jnp.mean(q * q, axis=0, keepdims=True) + EPSILON)
         k_scale = lax.rsqrt(jnp.mean(k * k, axis=0, keepdims=True) + EPSILON)
         q_hat, k_hat = q * q_scale, k * k_scale
@@ -133,24 +138,31 @@
         v_low = v.astype(BF16)
         if mixed_t is not None:
             out = jnp.dot(v_low, raised.astype(BF16), preferred_element_type=F32) * inverse
-            mixed_t[at[0], lanes] = out
+            stores.append((mixed_t, at[0], out))
         if dmixed_t is not None:
             weights = raised * inverse
-            d_out = dmixed_t[at[0], lanes].astype(BF16)
+            d_out = d_mixed.astype(BF16)
             d_weights = lax.dot_general(v_low, d_out, TN, preferred_element_type=F32)
             shift = jnp.sum(weights * d_weights, axis=0, keepdims=True)
             d_scores = (weights * (d_weights - shift)).astype(BF16)
-            dv = lax.dot_general(d_out, weights.astype(BF16), NT, preferred_element_type=F32)
+            dv = jnp.dot(weights.astype(BF16), d_out.T, preferred_element_type=F32).T
             dq = jnp.dot(k_high.astype(BF16), d_scores, preferred_element_type=F32)
-            dk = lax.dot_general(q_high.astype(BF16), d_scores, NT, preferred_element_type=F32)
+            dk = jnp.dot(d_scores, q_high.astype(BF16).T, preferred_element_type=F32).T
             dq = dq * (q_gain * root)
             dk = dk * k_gain
-            qkv_t[at[0], lanes] = q_scale * (dq - q_hat * jnp.mean(q_hat * dq, axis=0, keepdims=True))
-            qkv_t[at[1], lanes] = k_scale * (dk - k_hat * jnp.mean(k_hat * dk, axis=0, keepdims=True))
-            qkv_t[at[2], lanes] = dv
-        return carry
-
-    lax.fori_loop(0, 2 * HEADS, body, 0, unroll=2)
+            stores.append((qkv_t, at[0], q_scale * (dq - q_hat * jnp.mean(q_hat * dq, axis=0, keepdims=True))))
+            stores.append((qkv_t, at[1], k_scale * (dk - k_hat * jnp.mean(k_hat * dk, axis=0, keepdims=True))))
+            stores.append((qkv_t, at[2], dv))
+        return lanes, stores
+
+    def body(index, carry):
+        taken = [one(index * 4 + i // 2, i % 2) for i in range(8)]
+        for lanes, stores in [compute(*t) for t in taken]:
+            for ref, rows, value in stores:
+                ref[rows, lanes] = value
+        return carry
+
+    lax.fori_loop(first, last, body, 0, unroll=unroll)
 
 
 def wide_rows(source, used, ref):
@@ -192,15 +204,21 @@
         for t in range(size):
             work[(done + t) * MODEL:(done + t + 1) * MODEL, :] = out[:, t * 128:(t + 1) * 128]
         done += size
-    skip = max(0, 8 - tiles)
-
-    def gather(s, carry):
-        rows = [work[pl.ds(t * MODEL + 9 * s, 8), :] for t in range(tiles)]
-        rows.append(work[pl.ds(9 * s + 8, 8, stride=MODEL), :])
-        slab[s // 64, (s // 16) % 4, (s // 8) % 2, (s // 2) % 4, s % 2] = jnp.concatenate(rows, axis=0).astype(BF16)
-        return carry
-
-    lax.fori_loop(0, SHARDS, gather, 0, unroll=2)
+
+    pad = slab.shape[-2] - 8 * tiles - 8
+
+    def gather(wide, carry):
+        goal, base = slab.at[wide // 8, (wide // 2) % 4, wide % 2], pl.multiple_of(wide * 72, 8)
+        for narrow in range(8):
+            at = base + 9 * narrow
+            rows = [work[pl.ds(t * MODEL + at, 8), :] for t in range(tiles)]
+            rows.append(work[pl.ds(at + 8, 8, stride=MODEL), :])
+            if pad:
+                rows.append(jnp.zeros((pad, 128), F32))
+            goal[narrow // 2, narrow % 2] = jnp.concatenate(rows, axis=0).astype(BF16)
+        return carry
+
+    lax.fori_loop(0, SHARDS // 8, gather, 0)
 
 
 def pack_messages(source, send):
@@ -231,7 +249,7 @@
 
 def start_exchange(me, send, recv, send_sem, recv_sem, own_sem):
     def body(step, carry):
-        other = (me + step) % SHARDS
+        other = (me + step * 37) % SHARDS
         pltpu.make_async_remote_copy(
             src_ref=send.at[other], dst_ref=recv.at[me], send_sem=send_sem, recv_sem=recv_sem,
             device_id=(other // 8, other % 8), device_id_type=MESH).start()
@@ -360,6 +378,10 @@
         if level < 2:
             self.start(part, level + 1)
 
+    def drain_cores(self):
+        for part in range(COUNT):
+            self.flying.pop((part, "core")).wait_send()
+
     def drain(self):
         for made in self.flying.values():
             made.wait_send()
@@ -376,7 +398,7 @@
                 mixed_s, mixed_t, dqkv, left, work, tokens_a, tokens_b, send, recv_a, recv_b, slab0, slab1, slab2,
                 *rest):
     buffers = rest[:7 * COUNT]
-    load_sem, own_sem, send_a, send_b, got_a, got_b, sum_send, sum_recv, free_sem = rest[7 * COUNT:]
+    load_sem, own_sem, send_a, send_b, got_a, got_b, sum_send, sum_recv, free_sem, core_free = rest[7 * COUNT:]
     at = place()
     me = lax.axis_index("wide") * 8 + lax.axis_index("narrow")
     loads = []
@@ -426,11 +448,14 @@
     wide_rows(mixed_f, HD, mixed_t)
 
     def put_result(rows, value):
-        result[rows, :] = value.astype(BF16)
+        normed_t[rows, :] = value.astype(BF16)
 
     slabs = (slab0, slab1, slab2)
     sems = (sum_send, sum_recv)
+    partner = device_of(moved(at, "core", 1))
+    neighbours = [device_of(moved(at, a, d)) for a in ("x", "y", "z") for d in (1, 3)]
     sum_t = Scatter(at, slabs, buffers, sems, 0, sums, 1, scale)
+    sum_s = Scatter(at, slabs, buffers, sems, COUNT * 19, sums, 0, scale)
     left[...] = normed_t[...].T
     for part in (0, 1):
         gradient_part(left, dqkv, PARTS[part][0], PARTS[part][1], slabs[part], work)
@@ -439,49 +464,57 @@
     gradient_part(left, mixed_t, 0, PROJ_TILES, slabs[2], work)
     sum_t.begin(2)
     add_projection(middle, mixed_t, pt_t, adaln_t, put_result)
+    store_result = pltpu.make_async_copy(normed_t, result, load_sem.at[6])
+    store_result.start()
+    parts_step(sum_t.join_cores)
+    pl.semaphore_signal(core_free, inc=1, device_id=partner, device_id_type=MESH)
 
     own.wait()
     every.wait_recv()
+    parts_step(sum_t.relay, 0)
     unpack_messages(recv_b, tokens_b)
     d_middle = tile_rows(tokens_b)
     gate_cotangent(d_middle, adaln_s, branch)
     pull_mixed(pt_s, branch, dmixed_f)
-    parts_step(sum_t.join_cores)
-    heads_loop(qkv_s, gains_s, None, dmixed_f)
-    parts_step(sum_t.relay, 0)
+    parts_step(sum_t.finish, 0)
+    left[...] = branch[...].T
+    sum_t.drain_cores()
+    pl.semaphore_wait(core_free, 1)
+    gradient_part(left, mixed_s, 0, PROJ_TILES, slabs[2], work)
+    sum_s.begin(2)
+    parts_step(sum_t.relay, 1)
+    heads_loop(qkv_s, gains_s, None, dmixed_f, 0, 1)
+    parts_step(sum_t.finish, 1)
+    heads_loop(qkv_s, gains_s, None, dmixed_f, 1, 2)
+    parts_step(sum_t.relay, 2)
+
+    def put_grad(rows, value):
+        branch[rows, :] = value.astype(BF16)
+
     wide_rows(qkv_s, 3 * HD, dqkv)
-    parts_step(sum_t.finish, 0)
-
-    def put_grad(rows, value):
-        grad_clip[rows, :] = value.astype(BF16)
-
     left[...] = normed_s[...].T
-    parts_step(sum_t.relay, 1)
-    pull_norm(flat_rows(clip), d_middle, dqkv, wt_s, adaln_s, qkv_s, put_grad)
-    parts_step(sum_t.finish, 1)
-    parts_step(sum_t.relay, 2)
+    gradient_part(left, dqkv, PARTS[0][0], PARTS[0][1], slabs[0], work)
+    sum_s.begin(0)
     parts_step(sum_t.finish, 2)
     sum_t.drain()
-    peers = [device_of(moved(at, "core", 1))] + [device_of(moved(at, a, d)) for a in ("x", "y", "z") for d in (1, 3)]
-    for peer in peers:
+    for peer in neighbours:
         pl.semaphore_signal(free_sem, inc=1, device_id=peer, device_id_type=MESH)
-    sum_s = Scatter(at, slabs, buffers, sems, COUNT * 19, sums, 0, scale)
-    gradient_part(left, dqkv, PARTS[0][0], PARTS[0][1], slabs[0], work)
-    pl.semaphore_wait(free_sem, len(peers))
-    sum_s.begin(0)
     gradient_part(left, dqkv, PARTS[1][0], PARTS[1][1], slabs[1], work)
     sum_s.begin(1)
+    pl.semaphore_wait(free_sem, len(neighbours))
+    sum_s.join_cores(2)
     sum_s.join_cores(0)
-    left[...] = branch[...].T
-    gradient_part(left, mixed_s, 0, PROJ_TILES, slabs[2], work)
-    sum_s.begin(2)
     sum_s.join_cores(1)
-    sum_s.join_cores(2)
+    pull_norm(flat_rows(clip), d_middle, dqkv, wt_s, adaln_s, qkv_s, put_grad)
+    store_grad = pltpu.make_async_copy(branch, grad_clip, load_sem.at[7])
+    store_grad.start()
     for level in range(3):
         parts_step(sum_s.relay, level)
         parts_step(sum_s.finish, level)
     sum_s.drain()
     every.wait_send()
+    store_result.wait()
+    store_grad.wait()
 
 
 def split_sums(sums, qkv_s, proj_s, qkv_t, proj_t):
@@ -513,12 +546,12 @@
         functools.partial(both_blocks, scale),
         out_shape=[jax.ShapeDtypeStruct(*token), jax.ShapeDtypeStruct(*token), jax.ShapeDtypeStruct((2, 176, 128), F32)],
         in_specs=[hbm, hbm, hbm, hbm, vmem, vmem, hbm, hbm, vmem, vmem],
-        out_specs=[vmem] * 3,
+        out_specs=[hbm, hbm, vmem],
         scratch_shapes=[pltpu.VMEM(*s) for s in shapes] + [
-            pltpu.SemaphoreType.DMA((6,)), pltpu.SemaphoreType.DMA((2,)),
+            pltpu.SemaphoreType.DMA((8,)), pltpu.SemaphoreType.DMA((2,)),
             pltpu.SemaphoreType.DMA, pltpu.SemaphoreType.DMA, pltpu.SemaphoreType.DMA, pltpu.SemaphoreType.DMA,
             pltpu.SemaphoreType.DMA((2 * COUNT * 19,)), pltpu.SemaphoreType.DMA((2 * COUNT * 19,)),
-            pltpu.SemaphoreType.REGULAR],
+            pltpu.SemaphoreType.REGULAR, pltpu.SemaphoreType.REGULAR],
         compiler_params=pltpu.CompilerParams(collective_id=0, has_side_effects=True, vmem_limit_bytes=67043328),
         name="both_blocks",
     )(clip, cot, wt_s, pt_s, adaln_s, gains_s, wt_t, pt_t, adaln_t, gains_t)

time: 184 us -> 145 us (0.79)
  Pallas kernels: 176 us -> 137 us
    pallas_call x1, Pallas kernels: 174 us -> 135 us  [run_blocks(): pl.pallas_call(functools.partial(both_blocks, scale), out_shape=[jax.Shap...]
where the time goes in v1:
time: 145 us; the launch traced here: 144 us
  Pallas kernels  137 us (94%)
  local copies, waits for them, and re-layouts  7.02 us (5%)
    pallas_call x1, Pallas kernels, run_blocks(): pl.pallas_call(functools.partial(both_blocks, scale), out_shape=[jax.Shap...  135 us
    reshape x1, local copies, waits for them, and re-layouts, body(): result = jnp.transpose(result.reshape(2, SEQ, MODEL), (1, 0, 2))  3.59 us

profile of v1, /device:TPU:0, one launch (start us, length us, event | category | flops | bytes accessed | tf_op | source)
XLA Modules:
  0.0 144.4 jit_solution(967058980803171336)
XLA Ops:
  0.6 2.4 %copy.16 = bf16[2,256,1152]{2,1,0:T(8,128)(2,1)} copy(bf16[2,256,1152]{2,0,1:T(2,128)(2,1)} %bitcast.18) | data formatting | bytes 2359296 | tf_op jit(solution)/shard_map/transpose | solution.py:563
  3.0 135.1 %both_blocks.1 = (bf16[512,1152]{1,0:T(8,128)(2,1)}, bf16[512,1152]{1,0:T(8,128)(2,1)}, f32[2,176,128]{2,1,0:T(8,128)}) custom-call(bf16[512,1152]{1,0:T(8,128)(2,1)} %bitcast.17, bf16[512,1152]{1,0:T(8,128)(2,1)} %bitcast.12, bf16[1728,1152]{1,0:T(8,128)(2,1)} %bitcast.13, bf16[576,1152]{1,0:T(8,128)(2,1)} %bitcast.15, f32[3,1152]{1,0:T(4,128)} %adaln_s.1, ...), custom_call_target="tpu_custom_call" | custom-call | tf_op jit(solution)/shard_map/both_blocks/pallas_call | solution.py:545
  138.1 0.0 copy-start
  138.2 3.6 %copy.19 = bf16[2,256,1152]{2,0,1:T(2,128)(2,1)} copy(bf16[2,256,1152]{2,1,0:T(8,128)(2,1)} %bitcast.21) | data formatting | bytes 2359296 | tf_op jit(solution)/shard_map/reshape | solution.py:574
  141.7 1.6 %split_sums.1 = (f32[9,1728]{1,0:T(8,128)}, f32[9,576]{1,0:T(8,128)}, f32[9,1728]{1,0:T(8,128)}, f32[9,576]{1,0:T(8,128)}) custom-call(f32[2,176,128]{2,1,0:T(8,128)} %get-tuple-element.15.sums), custom_call_target="tpu_custom_call" | custom-call | tf_op jit(solution)/shard_map/split_sums/pallas_call | solution.py:567
  143.4 0.0 copy-done
  143.4 1.0 copy.21
Async XLA Ops:
  138.1 5.2 %copy-start = (bf16[512,1152]{1,0:T(8,128)(2,1)S(1)}, bf16[512,1152]{1,0:T(8,128)(2,1)}, u32[]{:S(2)}) copy-start(bf16[512,1152]{1,0:T(8,128)(2,1)} %get-tuple-element.14) | copy-start | bytes 3538948

commit v2 on v1

--- a/solution.py
+++ b/solution.py
@@ -221,6 +221,22 @@
     lax.fori_loop(0, SHARDS // 8, gather, 0)
 
 
+def split_pairs(pairs, tokens):
+    def body(rows):
+        for which in range(2):
+            tokens[pl.ds(pl.multiple_of(which * SEQ + rows.start, 16), 16), :] = pairs[rows, which, :]
+
+    row_loop(SEQ, 16, body)
+
+
+def join_pairs(tokens, pairs):
+    def body(rows):
+        for which in range(2):
+            pairs[rows, which, :] = tokens[pl.ds(pl.multiple_of(which * SEQ + rows.start, 16), 16), :]
+
+    row_loop(SEQ, 16, body)
+
+
 def pack_messages(source, send):
     top = lax.broadcasted_iota(jnp.int32, (8, 128), 0) < 2
 
@@ -375,13 +391,19 @@
             start = sum(p[2] for p in PARTS[:part])
             self.sums[self.which, start:start + PARTS[part][2], :] = (
                 source[...].astype(F32) + plus[...].astype(F32) + minus[...].astype(F32)) * self.scale
-        if level < 2:
-            self.start(part, level + 1)
 
     def drain_cores(self):
         for part in range(COUNT):
             self.flying.pop((part, "core")).wait_send()
 
+    def release(self, level, neighbours, free):
+        for part in range(COUNT):
+            for direction in (0, 1):
+                for kind in range(3):
+                    self.flying.pop((part, level, direction, kind)).wait_send()
+        for peer in neighbours:
+            pl.semaphore_signal(free.at[level], inc=1, device_id=peer, device_id_type=MESH)
+
     def drain(self):
         for made in self.flying.values():
             made.wait_send()
@@ -392,17 +414,23 @@
         step(part, *level)
 
 
+def next_level(scatter, level):
+    for part in range(COUNT):
+        scatter.finish(part, level)
+        scatter.start(part, level + 1)
+
+
 def both_blocks(scale, clip_hbm, cot_hbm, wt_s_hbm, pt_s_hbm, adaln_s, gains_s, wt_t_hbm, pt_t_hbm, adaln_t, gains_t,
                 result, grad_clip, sums,
-                clip, cot, wt_s, pt_s, wt_t, pt_t, normed_s, normed_t, branch, qkv_s, qkv_t, mixed_f, dmixed_f,
-                mixed_s, mixed_t, dqkv, left, work, tokens_a, tokens_b, send, recv_a, recv_b, slab0, slab1, slab2,
+                clip, pairs, cot, wt_s, pt_s, wt_t, pt_t, normed_s, normed_t, branch, qkv_s, qkv_t, mixed_f, dmixed_f,
+                mixed_s, mixed_t, dqkv, left, work, tokens_b, send, recv_a, recv_b, slab0, slab1, slab2,
                 *rest):
     buffers = rest[:7 * COUNT]
     load_sem, own_sem, send_a, send_b, got_a, got_b, sum_send, sum_recv, free_sem, core_free = rest[7 * COUNT:]
     at = place()
     me = lax.axis_index("wide") * 8 + lax.axis_index("narrow")
     loads = []
-    for i, (hbm, vmem) in enumerate(((clip_hbm, clip), (wt_s_hbm, wt_s), (pt_s_hbm, pt_s), (cot_hbm, cot),
+    for i, (hbm, vmem) in enumerate(((clip_hbm, clip), (wt_s_hbm, wt_s), (pt_s_hbm, pt_s), (cot_hbm, pairs),
                                      (pt_t_hbm, pt_t), (wt_t_hbm, wt_t))):
         load = pltpu.make_async_copy(hbm, vmem, load_sem.at[i])
         load.start()
@@ -423,12 +451,13 @@
     heads_loop(qkv_s, gains_s, mixed_f, None)
     wide_rows(mixed_f, HD, mixed_s)
     loads[2].wait()
-    add_projection(flat_rows(clip), mixed_s, pt_s, adaln_s, functools.partial(put_tiles, tokens_a))
-    pack_messages(tokens_a, send)
+    add_projection(flat_rows(clip), mixed_s, pt_s, adaln_s, functools.partial(put_tiles, work))
+    pack_messages(work, send)
     pl.semaphore_wait(barrier, SHARDS - 1)
     own, every = start_exchange(me, send, recv_a, send_a, got_a, own_sem.at[0])
 
     loads[3].wait()
+    split_pairs(pairs, cot)
     gate_cotangent(flat_rows(cot), adaln_t, branch)
     loads[4].wait()
     pull_mixed(pt_t, branch, dmixed_f)
@@ -441,9 +470,9 @@
     project_qkv(wt_t, normed_t, qkv_t)
     heads_loop(qkv_t, gains_t, mixed_f, dmixed_f)
     wide_rows(qkv_t, 3 * HD, dqkv)
-    pull_norm(middle, flat_rows(cot), dqkv, wt_t, adaln_t, qkv_t, functools.partial(put_tiles, tokens_a))
+    pull_norm(middle, flat_rows(cot), dqkv, wt_t, adaln_t, qkv_t, functools.partial(put_tiles, work))
     every.wait_send()
-    pack_messages(tokens_a, send)
+    pack_messages(work, send)
     own, every = start_exchange(me, send, recv_b, send_b, got_b, own_sem.at[1])
     wide_rows(mixed_f, HD, mixed_t)
 
@@ -464,29 +493,27 @@
     gradient_part(left, mixed_t, 0, PROJ_TILES, slabs[2], work)
     sum_t.begin(2)
     add_projection(middle, mixed_t, pt_t, adaln_t, put_result)
-    store_result = pltpu.make_async_copy(normed_t, result, load_sem.at[6])
+    join_pairs(normed_t, pairs)
+    store_result = pltpu.make_async_copy(pairs, result, load_sem.at[6])
     store_result.start()
+
+    own.wait()
+    every.wait_recv()
     parts_step(sum_t.join_cores)
     pl.semaphore_signal(core_free, inc=1, device_id=partner, device_id_type=MESH)
-
-    own.wait()
-    every.wait_recv()
-    parts_step(sum_t.relay, 0)
     unpack_messages(recv_b, tokens_b)
     d_middle = tile_rows(tokens_b)
     gate_cotangent(d_middle, adaln_s, branch)
     pull_mixed(pt_s, branch, dmixed_f)
-    parts_step(sum_t.finish, 0)
     left[...] = branch[...].T
     sum_t.drain_cores()
     pl.semaphore_wait(core_free, 1)
     gradient_part(left, mixed_s, 0, PROJ_TILES, slabs[2], work)
     sum_s.begin(2)
-    parts_step(sum_t.relay, 1)
-    heads_loop(qkv_s, gains_s, None, dmixed_f, 0, 1)
-    parts_step(sum_t.finish, 1)
-    heads_loop(qkv_s, gains_s, None, dmixed_f, 1, 2)
-    parts_step(sum_t.relay, 2)
+    parts_step(sum_t.relay, 0)
+    heads_loop(qkv_s, gains_s, None, dmixed_f)
+    next_level(sum_t, 0)
+    sum_t.release(0, neighbours, free_sem)
 
     def put_grad(rows, value):
         branch[rows, :] = value.astype(BF16)
@@ -495,22 +522,28 @@
     left[...] = normed_s[...].T
     gradient_part(left, dqkv, PARTS[0][0], PARTS[0][1], slabs[0], work)
     sum_s.begin(0)
-    parts_step(sum_t.finish, 2)
-    sum_t.drain()
-    for peer in neighbours:
-        pl.semaphore_signal(free_sem, inc=1, device_id=peer, device_id_type=MESH)
+    parts_step(sum_t.relay, 1)
     gradient_part(left, dqkv, PARTS[1][0], PARTS[1][1], slabs[1], work)
     sum_s.begin(1)
-    pl.semaphore_wait(free_sem, len(neighbours))
-    sum_s.join_cores(2)
-    sum_s.join_cores(0)
-    sum_s.join_cores(1)
+    pl.semaphore_wait(free_sem.at[0], len(neighbours))
+    for part in (2, 0, 1):
+        sum_s.join_cores(part)
+    next_level(sum_t, 1)
+    sum_t.release(1, neighbours, free_sem)
     pull_norm(flat_rows(clip), d_middle, dqkv, wt_s, adaln_s, qkv_s, put_grad)
     store_grad = pltpu.make_async_copy(branch, grad_clip, load_sem.at[7])
     store_grad.start()
-    for level in range(3):
-        parts_step(sum_s.relay, level)
-        parts_step(sum_s.finish, level)
+    parts_step(sum_t.relay, 2)
+    parts_step(sum_s.relay, 0)
+    parts_step(sum_t.finish, 2)
+    sum_t.release(2, neighbours, free_sem)
+    pl.semaphore_wait(free_sem.at[1], len(neighbours))
+    next_level(sum_s, 0)
+    parts_step(sum_s.relay, 1)
+    pl.semaphore_wait(free_sem.at[2], len(neighbours))
+    next_level(sum_s, 1)
+    parts_step(sum_s.relay, 2)
+    parts_step(sum_s.finish, 2)
     sum_s.drain()
     every.wait_send()
     store_result.wait()
@@ -535,23 +568,24 @@
     token, qkv_f, heads_f = ((TOKENS, MODEL), BF16), ((3 * HD, TOKENS), F32), ((HD, TOKENS), F32)
     tiles = ((LANE_TILES * TOKENS, 128), F32)
     mixed, message = ((TOKENS, PROJ_TILES * 128), BF16), ((SHARDS, MESSAGE, 128), BF16)
-    shapes = [token, token, ((3 * HD, MODEL), BF16), ((HD, MODEL), BF16), ((3 * HD, MODEL), BF16), ((HD, MODEL), BF16),
+    pairs = ((SEQ, 2, MODEL), BF16)
+    shapes = [token, pairs, token, ((3 * HD, MODEL), BF16), ((HD, MODEL), BF16), ((3 * HD, MODEL), BF16), ((HD, MODEL), BF16),
               token, token, token, qkv_f, qkv_f, heads_f, heads_f, mixed, mixed, ((TOKENS, QKV_TILES * 128), BF16),
-              ((MODEL, TOKENS), BF16), ((8 * MODEL, 128), F32), ((LANE_TILES * TOKENS + 8, 128), F32), tiles, message, message, message]
+              ((MODEL, TOKENS), BF16), ((8 * MODEL, 128), F32), tiles, message, message, message]
     shapes += [((2, 4, 2, 4, 2, rows, 128), BF16) for _, _, rows, _ in PARTS]
     for lead in ((2, 4, 4, 2), (4, 4, 4), (4, 4), (4,), (2, 2, 4, 4), (2, 2, 4), (2, 2)):
         shapes += [(lead + (rows, 128), BF16) for _, _, rows, _ in PARTS]
     vmem, hbm = pl.BlockSpec(memory_space=pltpu.VMEM), pl.BlockSpec(memory_space=pl.ANY)
     return pl.pallas_call(
         functools.partial(both_blocks, scale),
-        out_shape=[jax.ShapeDtypeStruct(*token), jax.ShapeDtypeStruct(*token), jax.ShapeDtypeStruct((2, 176, 128), F32)],
+        out_shape=[jax.ShapeDtypeStruct(*pairs), jax.ShapeDtypeStruct(*token), jax.ShapeDtypeStruct((2, 176, 128), F32)],
         in_specs=[hbm, hbm, hbm, hbm, vmem, vmem, hbm, hbm, vmem, vmem],
         out_specs=[hbm, hbm, vmem],
         scratch_shapes=[pltpu.VMEM(*s) for s in shapes] + [
             pltpu.SemaphoreType.DMA((8,)), pltpu.SemaphoreType.DMA((2,)),
             pltpu.SemaphoreType.DMA, pltpu.SemaphoreType.DMA, pltpu.SemaphoreType.DMA, pltpu.SemaphoreType.DMA,
             pltpu.SemaphoreType.DMA((2 * COUNT * 19,)), pltpu.SemaphoreType.DMA((2 * COUNT * 19,)),
-            pltpu.SemaphoreType.REGULAR, pltpu.SemaphoreType.REGULAR],
+            pltpu.SemaphoreType.REGULAR((3,)), pltpu.SemaphoreType.REGULAR],
         compiler_params=pltpu.CompilerParams(collective_id=0, has_side_effects=True, vmem_limit_bytes=67043328),
         name="both_blocks",
     )(clip, cot, wt_s, pt_s, adaln_s, gains_s, wt_t, pt_t, adaln_t, gains_t)
@@ -560,9 +594,8 @@
 def body(clip_tokens, cotangent, qkv_spatial, proj_spatial, adaln_spatial, qknorm_spatial,
          qkv_temporal, proj_temporal, adaln_temporal, qknorm_temporal):
     clip = clip_tokens.reshape(TOKENS, MODEL)
-    cot = jnp.transpose(cotangent, (1, 0, 2)).reshape(TOKENS, MODEL)
     result, grad_clip, sums = run_blocks(
-        1.0 / math.sqrt(SEQ * SEQ), clip, cot, qkv_spatial.T, proj_spatial.T, adaln_spatial, qknorm_spatial,
+        1.0 / math.sqrt(SEQ * SEQ), clip, cotangent, qkv_spatial.T, proj_spatial.T, adaln_spatial, qknorm_spatial,
         qkv_temporal.T, proj_temporal.T, adaln_temporal, qknorm_temporal)
     grads = pl.pallas_call(
         split_sums,
@@ -571,7 +604,6 @@
         out_specs=[pl.BlockSpec(memory_space=pltpu.VMEM)] * 4,
         name="split_sums",
     )(sums)
-    result = jnp.transpose(result.reshape(2, SEQ, MODEL), (1, 0, 2))
     return (result, grad_clip.reshape(2, SEQ, MODEL), *grads)
 
 

time: 145 us -> 144 us (level)
  local copies, waits for them, and re-layouts: 7.02 us -> 4.21 us
  Pallas kernels: 137 us -> 139 us
    reshape x1 -> x0, local copies, waits for them, and re-layouts: 3.59 us -> none  [body(): result = jnp.transpose(result.reshape(2, SEQ, MODEL), (1, 0, 2))]
    unnamed x3 -> x4, local copies, waits for them, and re-layouts: 1.02 us -> 4.21 us
    transpose x1 -> x0, local copies, waits for them, and re-layouts: 2.41 us -> none  [body(): cot = jnp.transpose(cotangent, (1, 0, 2)).reshape(TOKENS, MODEL)]
    pallas_call x1, Pallas kernels: 135 us -> 137 us  [run_blocks(): pl.pallas_call(functools.partial(both_blocks, scale), out_shape=[jax.Shap...]
where the time goes in v2:
time: 144 us
  Pallas kernels  139 us (97%)
  local copies, waits for them, and re-layouts  4.21 us (3%)
    pallas_call x1, Pallas kernels, run_blocks(): pl.pallas_call(functools.partial(both_blocks, scale), out_shape=[jax.Shap...  137 us
    unnamed x4, local copies, waits for them, and re-layouts  4.21 us

profile of v2, /device:TPU:0, one launch (start us, length us, event | category | flops | bytes accessed | tf_op | source)
XLA Modules:
  0.0 143.8 jit_solution(6623460987486834408)
XLA Ops:
  0.6 137.3 %both_blocks.1 = (bf16[256,2,1152]{2,1,0:T(2,128)(2,1)}, bf16[512,1152]{1,0:T(8,128)(2,1)}, f32[2,176,128]{2,1,0:T(8,128)}) custom-call(bf16[512,1152]{1,0:T(8,128)(2,1)} %bitcast.10, bf16[256,2,1152]{2,1,0:T(2,128)(2,1)} %cot_hbm.1, bf16[1728,1152]{1,0:T(8,128)(2,1)} %bitcast.6, bf16[576,1152]{1,0:T(8,128)(2,1)} %bitcast.8, f32[3,1152]{1,0:T(4,128)} %adaln_s.1, ...), custom_call_target="tpu_custom_call" | custom-call | tf_op jit(solution)/shard_map/both_blocks/pallas_call | solution.py:579
  137.9 1.6 %split_sums.1 = (f32[9,1728]{1,0:T(8,128)}, f32[9,576]{1,0:T(8,128)}, f32[9,1728]{1,0:T(8,128)}, f32[9,576]{1,0:T(8,128)}) custom-call(f32[2,176,128]{2,1,0:T(8,128)} %get-tuple-element.15.sums), custom_call_target="tpu_custom_call" | custom-call | tf_op jit(solution)/shard_map/split_sums/pallas_call | solution.py:600
  139.6 0.0 copy-start
  139.6 3.2 %copy.18 = bf16[256,2,1152]{2,1,0:T(2,128)(2,1)} copy(bf16[256,2,1152]{2,1,0:T(2,128)(2,1)} %get-tuple-element.26) | data formatting | bytes 2359296
  142.8 0.0 copy-done
  142.8 1.0 copy.19
Async XLA Ops:
  139.6 3.2 %copy-start = (bf16[512,1152]{1,0:T(8,128)(2,1)S(1)}, bf16[512,1152]{1,0:T(8,128)(2,1)}, u32[]{:S(2)}) copy-start(bf16[512,1152]{1,0:T(8,128)(2,1)} %get-tuple-element.14) | copy-start | bytes 3538948

commit v3 on v2

--- a/solution.py
+++ b/solution.py
@@ -195,7 +195,7 @@
     row_loop(TOKENS, 16, body, 4)
 
 
-def gradient_part(left, right, first_tile, tiles, slab, work):
+def gradient_part(left, right, first_tile, tiles, slab, work, beside=None):
     done = 0
     while done < tiles:
         size = min(2, tiles - done)
@@ -204,6 +204,8 @@
         for t in range(size):
             work[(done + t) * MODEL:(done + t + 1) * MODEL, :] = out[:, t * 128:(t + 1) * 128]
         done += size
+        if beside is not None:
+            beside()
 
     pad = slab.shape[-2] - 8 * tiles - 8
 
@@ -221,8 +223,9 @@
     lax.fori_loop(0, SHARDS // 8, gather, 0)
 
 
-def split_pairs(pairs, tokens):
+def split_pairs(pairs, tokens, beside):
     def body(rows):
+        beside(rows.start // 16)
         for which in range(2):
             tokens[pl.ds(pl.multiple_of(which * SEQ + rows.start, 16), 16), :] = pairs[rows, which, :]
 
@@ -263,22 +266,34 @@
     lax.fori_loop(0, SHARDS, body, 0, unroll=4)
 
 
-def start_exchange(me, send, recv, send_sem, recv_sem, own_sem):
-    def body(step, carry):
-        other = (me + step * 37) % SHARDS
+class Exchange:
+    def __init__(self, me, send, recv, send_sem, recv_sem, own_sem):
+        self.me, self.send, self.recv, self.sems = me, send, recv, (send_sem, recv_sem)
+        self.own = pltpu.make_async_copy(send.at[me], recv.at[me], own_sem)
+        self.next = 1
+
+    def one(self, step):
+        other = (self.me + step * 37) % SHARDS
         pltpu.make_async_remote_copy(
-            src_ref=send.at[other], dst_ref=recv.at[me], send_sem=send_sem, recv_sem=recv_sem,
+            src_ref=self.send.at[other], dst_ref=self.recv.at[self.me], send_sem=self.sems[0], recv_sem=self.sems[1],
             device_id=(other // 8, other % 8), device_id_type=MESH).start()
-        return carry
-
-    lax.fori_loop(1, SHARDS, body, 0)
-    own = pltpu.make_async_copy(send.at[me], recv.at[me], own_sem)
-    own.start()
-    every = pltpu.make_async_remote_copy(
-        src_ref=send.at[pl.ds(0, SHARDS - 1)], dst_ref=recv.at[pl.ds(0, SHARDS - 1)],
-        send_sem=send_sem, recv_sem=recv_sem, device_id=((me + 1) % SHARDS // 8, (me + 1) % SHARDS % 8),
-        device_id_type=MESH)
-    return own, every
+
+    def some(self, count):
+        first, self.next = self.next, min(self.next + count, SHARDS)
+        lax.fori_loop(first, self.next, lambda step, c: (self.one(step), c)[1], 0)
+
+    def every(self):
+        other = (self.me + 1) % SHARDS
+        return pltpu.make_async_remote_copy(
+            src_ref=self.send.at[pl.ds(0, SHARDS - 1)], dst_ref=self.recv.at[pl.ds(0, SHARDS - 1)],
+            send_sem=self.sems[0], recv_sem=self.sems[1], device_id=(other // 8, other % 8), device_id_type=MESH)
+
+    def wait_recv(self):
+        self.own.wait()
+        self.every().wait_recv()
+
+    def wait_send(self):
+        self.every().wait_send()
 
 
 def add_rows(count, target, sources):
@@ -454,16 +469,24 @@
     add_projection(flat_rows(clip), mixed_s, pt_s, adaln_s, functools.partial(put_tiles, work))
     pack_messages(work, send)
     pl.semaphore_wait(barrier, SHARDS - 1)
-    own, every = start_exchange(me, send, recv_a, send_a, got_a, own_sem.at[0])
+    first = Exchange(me, send, recv_a, send_a, got_a, own_sem.at[0])
+    first.own.start()
+    first.some(8)
+
+    def seven(index):
+        for i in range(7):
+            first.one(9 + index * 7 + i)
+
 
     loads[3].wait()
-    split_pairs(pairs, cot)
+    split_pairs(pairs, cot, seven)
+    first.next = 121
+    first.some(7)
     gate_cotangent(flat_rows(cot), adaln_t, branch)
     loads[4].wait()
     pull_mixed(pt_t, branch, dmixed_f)
     loads[5].wait()
-    own.wait()
-    every.wait_recv()
+    first.wait_recv()
     unpack_messages(recv_a, tokens_b)
     middle = tile_rows(tokens_b)
     norm_tokens(middle, adaln_t, normed_t)
@@ -471,9 +494,11 @@
     heads_loop(qkv_t, gains_t, mixed_f, dmixed_f)
     wide_rows(qkv_t, 3 * HD, dqkv)
     pull_norm(middle, flat_rows(cot), dqkv, wt_t, adaln_t, qkv_t, functools.partial(put_tiles, work))
-    every.wait_send()
+    first.wait_send()
     pack_messages(work, send)
-    own, every = start_exchange(me, send, recv_b, send_b, got_b, own_sem.at[1])
+    second = Exchange(me, send, recv_b, send_b, got_b, own_sem.at[1])
+    second.own.start()
+    second.some(12)
     wide_rows(mixed_f, HD, mixed_t)
 
     def put_result(rows, value):
@@ -487,18 +512,18 @@
     sum_s = Scatter(at, slabs, buffers, sems, COUNT * 19, sums, 0, scale)
     left[...] = normed_t[...].T
     for part in (0, 1):
-        gradient_part(left, dqkv, PARTS[part][0], PARTS[part][1], slabs[part], work)
+        gradient_part(left, dqkv, PARTS[part][0], PARTS[part][1], slabs[part], work, lambda: second.some(11))
         sum_t.begin(part)
     left[...] = branch[...].T
-    gradient_part(left, mixed_t, 0, PROJ_TILES, slabs[2], work)
+    gradient_part(left, mixed_t, 0, PROJ_TILES, slabs[2], work, lambda: second.some(9))
+    second.some(SHARDS)
     sum_t.begin(2)
     add_projection(middle, mixed_t, pt_t, adaln_t, put_result)
     join_pairs(normed_t, pairs)
     store_result = pltpu.make_async_copy(pairs, result, load_sem.at[6])
     store_result.start()
 
-    own.wait()
-    every.wait_recv()
+    second.wait_recv()
     parts_step(sum_t.join_cores)
     pl.semaphore_signal(core_free, inc=1, device_id=partner, device_id_type=MESH)
     unpack_messages(recv_b, tokens_b)
@@ -545,12 +570,19 @@
     parts_step(sum_s.relay, 2)
     parts_step(sum_s.finish, 2)
     sum_s.drain()
-    every.wait_send()
+    second.wait_send()
     store_result.wait()
     store_grad.wait()
 
 
-def split_sums(sums, qkv_s, proj_s, qkv_t, proj_t):
+def split_sums(sums, result, grad_clip, qkv_s, proj_s, qkv_t, proj_t, result_out, grad_out, pairs, tokens, sems):
+    taken = [pltpu.make_async_copy(result, pairs, sems.at[0]), pltpu.make_async_copy(grad_clip, tokens, sems.at[1])]
+    given = [pltpu.make_async_copy(pairs, result_out, sems.at[2]), pltpu.make_async_copy(tokens, grad_out, sems.at[3])]
+    for copy in taken:
+        copy.start()
+    for come, go in zip(taken, given):
+        come.wait()
+        go.start()
     for which, outs in enumerate(((qkv_s, proj_s), (qkv_t, proj_t))):
         start = 0
         for first, tiles, rows, _ in PARTS:
@@ -562,6 +594,8 @@
                 ninth = start + 8 * tiles + t
                 out[8:9, lane:lane + width] = sums[which, ninth:ninth + 1, :width]
             start += rows
+    for copy in given:
+        copy.wait()
 
 
 def run_blocks(scale, clip, cot, wt_s, pt_s, adaln_s, gains_s, wt_t, pt_t, adaln_t, gains_t):
@@ -597,13 +631,17 @@
     result, grad_clip, sums = run_blocks(
         1.0 / math.sqrt(SEQ * SEQ), clip, cotangent, qkv_spatial.T, proj_spatial.T, adaln_spatial, qknorm_spatial,
         qkv_temporal.T, proj_temporal.T, adaln_temporal, qknorm_temporal)
-    grads = pl.pallas_call(
+    token, pairs = ((TOKENS, MODEL), BF16), ((SEQ, 2, MODEL), BF16)
+    vmem, hbm = pl.BlockSpec(memory_space=pltpu.VMEM), pl.BlockSpec(memory_space=pl.ANY)
+    *grads, result, grad_clip = pl.pallas_call(
         split_sums,
-        out_shape=[jax.ShapeDtypeStruct((9, 3 * HD), F32), jax.ShapeDtypeStruct((9, HD), F32)] * 2,
-        in_specs=[pl.BlockSpec(memory_space=pltpu.VMEM)],
-        out_specs=[pl.BlockSpec(memory_space=pltpu.VMEM)] * 4,
+        out_shape=[jax.ShapeDtypeStruct((9, 3 * HD), F32), jax.ShapeDtypeStruct((9, HD), F32)] * 2 + [
+            jax.ShapeDtypeStruct(*pairs), jax.ShapeDtypeStruct(*token)],
+        in_specs=[vmem, hbm, hbm],
+        out_specs=[vmem] * 4 + [hbm] * 2,
+        scratch_shapes=[pltpu.VMEM(*pairs), pltpu.VMEM(*token), pltpu.SemaphoreType.DMA((4,))],
         name="split_sums",
-    )(sums)
+    )(sums, result, grad_clip)
     return (result, grad_clip.reshape(2, SEQ, MODEL), *grads)
 
 

time: 144 us -> 142 us (0.986)
  local copies, waits for them, and re-layouts: 4.21 us -> 0 us
  Pallas kernels: 139 us -> 141 us
    unnamed x4 -> x0, local copies, waits for them, and re-layouts: 4.21 us -> none
    pallas_call x1, Pallas kernels: 1.64 us -> 4.33 us  [body(): pl.pallas_call(split_sums, out_shape=[jax.ShapeDtypeStruct((9, 3 * HD), F...]
where the time goes in v3:
time: 142 us
  Pallas kernels  141 us (99%)
    pallas_call x1, Pallas kernels, run_blocks(): pl.pallas_call(functools.partial(both_blocks, scale), out_shape=[jax.Shap...  137 us
    pallas_call x1, Pallas kernels, body(): pl.pallas_call(split_sums, out_shape=[jax.ShapeDtypeStruct((9, 3 * HD), F...  4.33 us

profile of v3, /device:TPU:0, one launch (start us, length us, event | category | flops | bytes accessed | tf_op | source)
XLA Modules:
  0.0 142.2 jit_solution(13524424157042792323)
XLA Ops:
  0.6 137.0 %both_blocks.1 = (bf16[256,2,1152]{2,1,0:T(2,128)(2,1)}, bf16[512,1152]{1,0:T(8,128)(2,1)}, f32[2,176,128]{2,1,0:T(8,128)}) custom-call(bf16[512,1152]{1,0:T(8,128)(2,1)} %bitcast.10, bf16[256,2,1152]{2,1,0:T(2,128)(2,1)} %cot_hbm.1, bf16[1728,1152]{1,0:T(8,128)(2,1)} %bitcast.6, bf16[576,1152]{1,0:T(8,128)(2,1)} %bitcast.8, f32[3,1152]{1,0:T(4,128)} %adaln_s.1, ...), custom_call_target="tpu_custom_call" | custom-call | tf_op jit(solution)/shard_map/both_blocks/pallas_call | solution.py:613
  137.7 4.3 %split_sums.1 = (f32[9,1728]{1,0:T(8,128)}, f32[9,576]{1,0:T(8,128)}, f32[9,1728]{1,0:T(8,128)}, f32[9,576]{1,0:T(8,128)}, bf16[256,2,1152]{2,1,0:T(2,128)(2,1)}, /*index=5*/bf16[512,1152]{1,0:T(8,128)(2,1)}) custom-call(f32[2,176,128]{2,1,0:T(8,128)} %get-tuple-element.15.sums, bf16[256,2,1152]{2,1,0:T(2,128)(2,1)} %get-tuple-element.16.result, ...), custom_call_target="tpu_custom_call" | custom-call | tf_op jit(solution)/shard_map/split_sums/pallas_call | solution.py:636
